TPU v7x, 32 devices: a whole 2x2x4 slice. The times are simulated.
32 devices in a mesh: dp: 4 (over y, core), mp: 8 (over z, x).
Axes of the slice: x: 2, y: 2, z: 4, core: 2. Of those that a mesh axis runs over, the one named last changes fastest.
Arguments:
- query_rows: bfloat16 [8192, 16, 128], P('dp', 'mp'), may hold values from -8 to 8
- key_rows: bfloat16 [8192, 16, 128], P('dp', 'mp'), may hold values from -8 to 8
- value_rows: bfloat16 [8192, 16, 128], P('dp', 'mp'), may hold values from -6 to 6
- residual: bfloat16 [4096, 8, 768], P('dp', 'mp'), may hold values from -40 to 40
- lengths: int32 [64], replicated, may hold values from 1 to 256, as said below
- assignment: int32 [64], replicated, may hold values from 0 to 3, as said below
- out_proj: bfloat16 [1024, 1536], P(None, 'mp'), may hold values from -0.1875 to 0.1875
- norm_gain: float32 [1536], replicated, may hold values from 0.5 to 1.5
- norm_bias: float32 [1536], replicated, may hold values from -3 to 3
- glu_proj: bfloat16 [1536, 3072], P(None, 'mp'), may hold values from -0.15625 to 0.15625
- conv_taps: float32 [31, 1536], replicated, may hold values from -1 to 1
- batch_scale: float32 [1536], replicated, may hold values from 0.25 to 1.75
- batch_shift: float32 [1536], replicated, may hold values from -3 to 3
- down_proj: bfloat16 [1536, 1536], P(None, 'mp'), may hold values from -0.15625 to 0.15625
Outputs:
- encoded: bfloat16 [16384, 1536], P(('dp', 'mp'))
Inputs may be any that keep to these rules, and one draw needn't show every extreme that they name: `lengths`: utterance u starts in data group u // 16; a data group holds its utterances in order of u from its first frame on, and its frames after them are padding. In every draw every data group sends exactly 256 frames in each of its 4 utterances to one and the same data group, so that this group receives 4 * 256 frames from every data group; the utterances one data group sends to one data group never have more frames together. `assignment`: every data group sends exactly 4 of its utterances to each data group, itself included. In its new group an utterance lies after those of lower number, from the first frame on, and the frames after them are padding.
All inputs are finite; a program needn't handle non-finite values.
Results may differ from a plain program's by a relative error of at most 0.0034.
Values may be sent and summed in bfloat16 or wider, within the bound.
A program may use at most 128 MiB of HBM per device.

v0:
```python
import functools

import jax
import jax.numpy as jnp
from jax import lax
from jax.experimental import pallas as pl
from jax.experimental.pallas import tpu as pltpu
from jax.sharding import PartitionSpec as P

HD = 64
KERNEL = 31
HALF = 15
MAXLEN = 256
PIECES = 4
LANES = 128
HALO = 16
CONV_ROWS = 64

EPS = 1e-05
MASKED = -1e30
VMEM_LIMIT = 60 * 1024 * 1024


def params():
    return pltpu.CompilerParams(vmem_limit_bytes=VMEM_LIMIT)


def whole_spec():
    return pl.BlockSpec(memory_space=pltpu.VMEM)


def smem_spec():
    return pl.BlockSpec(memory_space=pltpu.SMEM)


def attention_kernel(
    heads, start_ref, span_ref, q_ref, k_ref, v_ref, out_ref, q_rows, k_rows, v_rows
):
    pairs = q_ref.shape[0]
    step = 256
    lane = lax.broadcasted_iota(jnp.int32, (step, LANES), 1)
    low = lane < HD

    def unpack(chunk, carry):
        first = pl.multiple_of(chunk * step, step)
        for packed, rows in ((q_ref, q_rows), (k_ref, k_rows), (v_ref, v_rows)):
            one = packed[pl.ds(first, step), 0:LANES].astype(jnp.float32)
            if heads == 2:
                two = packed[pl.ds(first, step), LANES : 2 * LANES].astype(jnp.float32)
                even = jnp.where(low, one, pltpu.roll(two, HD, 1))
                odd = jnp.where(low, pltpu.roll(one, HD, 1), two)
            else:
                even = one
                odd = pltpu.roll(one, HD, 1)
            rows[pl.ds(2 * first, step, stride=2), :] = even
            rows[pl.ds(2 * first + 1, step, stride=2), :] = odd
        return carry

    lax.fori_loop(0, pairs // step, unpack, 0)
    for rows in (q_rows, k_rows, v_rows):
        rows[pl.ds(2 * pairs, MAXLEN), :] = jnp.zeros((MAXLEN, LANES), jnp.float32)

    column = lax.broadcasted_iota(jnp.int32, (MAXLEN, MAXLEN), 1)
    head_lane = lax.broadcasted_iota(jnp.int32, (MAXLEN, LANES), 1) // HD

    def slot_body(slot, carry):
        start = start_ref[slot]
        allowed = column < span_ref[slot]
        queries = q_rows[pl.ds(start, MAXLEN), :]
        keys = k_rows[pl.ds(start, MAXLEN), :].astype(jnp.bfloat16)
        values = v_rows[pl.ds(start, MAXLEN), :].astype(jnp.bfloat16)
        result = None
        for head in range(heads):
            own = jnp.where(head_lane == head, queries, 0.0).astype(jnp.bfloat16)
            scores = (
                lax.dot_general(
                    own, keys, (((1,), (1,)), ((), ())), preferred_element_type=jnp.float32
                )
                * HD ** (-0.5)
            )
            scores = jnp.where(allowed, scores, MASKED)
            highest = jnp.max(scores, axis=1, keepdims=True)
            exponentials = jnp.exp(scores - highest)
            denominator = jnp.sum(exponentials, axis=1, keepdims=True)
            weights = (exponentials / denominator).astype(jnp.bfloat16)
            blended = jnp.dot(weights, values, preferred_element_type=jnp.float32)
            result = blended if head == 0 else jnp.where(head_lane == head, blended, result)
        out_ref[slot] = result[:, : heads * HD].astype(jnp.bfloat16)
        return carry

    lax.fori_loop(0, start_ref.shape[0], slot_body, 0)


def attend(start, span, query_rows, key_rows, value_rows):
    pairs, heads, _ = query_rows.shape
    slots = start.shape[0]
    flat = [a.reshape(pairs, heads * LANES) for a in (query_rows, key_rows, value_rows)]
    return pl.pallas_call(
        functools.partial(attention_kernel, heads),
        out_shape=jax.ShapeDtypeStruct((slots, MAXLEN, heads * HD), jnp.bfloat16),
        in_specs=[smem_spec()] * 2 + [whole_spec()] * 3,
        out_specs=whole_spec(),
        scratch_shapes=[pltpu.VMEM((2 * pairs + MAXLEN, LANES), jnp.float32)] * 3,
        compiler_params=params(),
        cost_estimate=pl.CostEstimate(
            flops=slots * heads * MAXLEN * MAXLEN * LANES * 4,
            bytes_accessed=pairs * heads * LANES * 8,
            transcendentals=slots * heads * MAXLEN * MAXLEN,
        ),
    )(start, span, *flat)


def lane_tiles(width):
    return [(first, min(LANES, width - first)) for first in range(0, width, LANES)]


def slots_kernel(start_ref, rows_ref, out_ref, *held):
    count, width = rows_ref.shape
    for (first, size), rows in zip(lane_tiles(width), held):

        def widen(chunk, carry):
            at = pl.multiple_of(chunk * MAXLEN, MAXLEN)
            rows[pl.ds(at, MAXLEN), 0:size] = rows_ref[
                pl.ds(at, MAXLEN), first : first + size
            ].astype(jnp.float32)
            return carry

        lax.fori_loop(0, count // MAXLEN, widen, 0)
        rows[pl.ds(count, MAXLEN), :] = jnp.zeros((MAXLEN, LANES), jnp.float32)

    def slot_body(slot, carry):
        start = start_ref[slot]
        for (first, size), rows in zip(lane_tiles(width), held):
            taken = rows[pl.ds(start, MAXLEN), :]
            out_ref[slot, :, first : first + size] = taken[:, :size].astype(jnp.bfloat16)
        return carry

    lax.fori_loop(0, start_ref.shape[0], slot_body, 0)


def into_slots(start, rows):
    count, width = rows.shape
    slots = start.shape[0]
    return pl.pallas_call(
        slots_kernel,
        out_shape=jax.ShapeDtypeStruct((slots, MAXLEN, width), jnp.bfloat16),
        in_specs=[smem_spec(), whole_spec()],
        out_specs=whole_spec(),
        scratch_shapes=[pltpu.VMEM((count + MAXLEN, LANES), jnp.float32)] * len(lane_tiles(width)),
        compiler_params=params(),
    )(start, rows)


def place_kernel(after_ref, slots_ref, out_ref, *held):
    slots, _, width = slots_ref.shape
    slabs, tall, _ = out_ref.shape
    slab_rows = tall - 2 * HALO
    total_rows = held[0].shape[0]
    zeros = jnp.zeros((MAXLEN, LANES), jnp.float32)
    for (first, size), rows in zip(lane_tiles(width), held):
        rows[pl.ds(0, HALO), :] = jnp.zeros((HALO, LANES), jnp.float32)

        def put(slot, carry):
            rows[pl.ds(HALO + after_ref[slot], MAXLEN), 0:size] = slots_ref[
                slot, :, first : first + size
            ].astype(jnp.float32)
            return carry

        lax.fori_loop(0, slots, put, 0)
        live = after_ref[slots]

        def clear(step, carry):
            at = jnp.minimum(HALO + live + step * MAXLEN, total_rows - MAXLEN)
            rows[pl.ds(at, MAXLEN), :] = zeros
            return carry

        lax.fori_loop(0, (total_rows - HALO - live + MAXLEN - 1) // MAXLEN, clear, 0)

        def emit(slab, carry):
            at = pl.multiple_of(slab * slab_rows, slab_rows)
            taken = rows[pl.ds(at, tall), :]
            out_ref[slab, :, first : first + size] = taken[:, :size].astype(jnp.bfloat16)
            return carry

        lax.fori_loop(0, slabs, emit, 0)


def place(after, slots, slabs, slab_rows):
    count, _, width = slots.shape
    return pl.pallas_call(
        place_kernel,
        out_shape=jax.ShapeDtypeStruct((slabs, slab_rows + 2 * HALO, width), jnp.bfloat16),
        in_specs=[smem_spec(), whole_spec()],
        out_specs=whole_spec(),
        scratch_shapes=[pltpu.VMEM((count * MAXLEN + HALO + MAXLEN, LANES), jnp.float32)]
        * len(lane_tiles(width)),
        compiler_params=params(),
    )(after, slots)


def conv_kernel(
    uniform_ref, gated_ref, segment_ref, taps_ref, scale_ref, shift_ref, out_ref, wide
):
    wide[...] = gated_ref[...].astype(jnp.float32)
    edge = HALO - HALF
    scale = scale_ref[...]
    shift = shift_ref[...]
    for chunk in range(out_ref.shape[0] // CONV_ROWS):
        base = chunk * CONV_ROWS

        def finish(total):
            affine = total * scale + shift
            out_ref[base : base + CONV_ROWS, :] = (affine * jax.nn.sigmoid(affine)).astype(
                jnp.bfloat16
            )

        @pl.when(uniform_ref[chunk] == 1)
        def _():
            total = jnp.zeros((CONV_ROWS, LANES), jnp.float32)
            for tap in range(KERNEL):
                total = total + wide[pl.ds(base + edge + tap, CONV_ROWS), :] * taps_ref[
                    tap : tap + 1, :
                ]
            finish(total)

        @pl.when(uniform_ref[chunk] == 0)
        def _():
            centre = segment_ref[pl.ds(base + HALO, CONV_ROWS), :]
            total = jnp.zeros((CONV_ROWS, LANES), jnp.float32)
            for tap in range(KERNEL):
                same = segment_ref[pl.ds(base + edge + tap, CONV_ROWS), :] == centre
                term = jnp.where(same, wide[pl.ds(base + edge + tap, CONV_ROWS), :], 0.0)
                total = total + term * taps_ref[tap : tap + 1, :]
            finish(total)


def convolve(gated_rows, segment, conv_taps, batch_scale, batch_shift):
    tall, width = gated_rows.shape
    rows = tall - 2 * HALO
    chunks = rows // CONV_ROWS
    windows = [segment[c * CONV_ROWS : c * CONV_ROWS + CONV_ROWS + 2 * HALO] for c in range(chunks)]
    windows = jnp.stack(windows)
    uniform = jnp.all(windows == windows[:, :1], axis=1).astype(jnp.int32)
    wide_segment = jnp.broadcast_to(segment[:, None], (tall, LANES))
    return pl.pallas_call(
        conv_kernel,
        grid=(width // LANES,),
        out_shape=jax.ShapeDtypeStruct((rows, width), jnp.bfloat16),
        in_specs=[
            smem_spec(),
            pl.BlockSpec((tall, LANES), lambda i: (0, i)),
            pl.BlockSpec((tall, LANES), lambda i: (0, 0)),
            pl.BlockSpec((KERNEL, LANES), lambda i: (0, i)),
            pl.BlockSpec((1, LANES), lambda i: (0, i)),
            pl.BlockSpec((1, LANES), lambda i: (0, i)),
        ],
        out_specs=pl.BlockSpec((rows, LANES), lambda i: (0, i)),
        scratch_shapes=[pltpu.VMEM((tall, LANES), jnp.float32)],
        compiler_params=params(),
        cost_estimate=pl.CostEstimate(
            flops=2 * rows * width * KERNEL, bytes_accessed=4 * rows * width, transcendentals=0
        ),
    )(
        uniform,
        gated_rows,
        wide_segment,
        conv_taps,
        batch_scale[None, :],
        batch_shift[None, :],
    )


def on_device(
    query_rows,
    key_rows,
    value_rows,
    residual,
    lengths,
    assignment,
    out_proj,
    norm_gain,
    norm_bias,
    glu_proj,
    conv_taps,
    batch_scale,
    batch_shift,
    down_proj,
):
    data_group = lax.axis_index("dp")
    slab_index = lax.axis_index("mp")
    groups = lax.axis_size("dp")
    slabs = lax.axis_size("mp")
    group_rows = query_rows.shape[0] * 2
    slab_rows = group_rows // slabs
    total_utterances = lengths.shape[0]
    per_group = total_utterances // groups
    slots = groups * PIECES
    features = residual.shape[2] // 4

    utterance = jnp.arange(total_utterances, dtype=jnp.int32)
    source = utterance // per_group
    earlier = utterance[None, :] < utterance[:, None]
    same_source = source[None, :] == source[:, None]
    same_target = assignment[None, :] == assignment[:, None]
    before = jnp.sum(jnp.where(earlier & same_source, lengths[None, :], 0), axis=1)
    rank = jnp.sum((earlier & same_source & same_target).astype(jnp.int32), axis=1)
    slot = jnp.arange(slots, dtype=jnp.int32)[:, None]
    leaving = (source[None, :] == data_group) & ((assignment * PIECES + rank)[None, :] == slot)
    start = jnp.sum(jnp.where(leaving, before[None, :], 0), axis=1)
    span = jnp.sum(jnp.where(leaving, lengths[None, :], 0), axis=1)
    coming = (assignment[None, :] == data_group) & ((source * PIECES + rank)[None, :] == slot)
    coming_earlier = (assignment[None, :] == data_group) & (
        (source * PIECES + rank)[None, :] < jnp.arange(slots + 1, dtype=jnp.int32)[:, None]
    )
    after = jnp.sum(jnp.where(coming_earlier, lengths[None, :], 0), axis=1)
    live = jnp.sum(jnp.where(assignment == data_group, lengths, 0))

    position = jnp.arange(slab_rows + 2 * HALO, dtype=jnp.int32) + slab_index * slab_rows - HALO
    segment = jnp.sum((position[:, None] >= after[None, 1:]).astype(jnp.int32), axis=1)
    segment = jnp.where(position < 0, -2, jnp.where(position < live, segment, -1))
    segment = jnp.where(position >= group_rows, -2, segment)

    residual_rows = (
        residual.reshape(group_rows // 4, 4, features).reshape(group_rows, features)
    )

    def swap(array, axis):
        return lax.all_to_all(array, axis, split_axis=0, concat_axis=0, tiled=True)

    def carry_over(array):
        placed = place(after, swap(array, "dp"), slabs, slab_rows)
        return swap(placed, "mp").transpose(1, 0, 2).reshape(slab_rows + 2 * HALO, -1)

    carried_slab = carry_over(into_slots(start, residual_rows))
    context_slab = carry_over(attend(start, span, query_rows, key_rows, value_rows))

    def gather(weights):
        return lax.all_gather(weights, "mp", axis=1, tiled=True)

    carried = carried_slab.astype(jnp.float32) + jnp.dot(
        context_slab, gather(out_proj), preferred_element_type=jnp.float32
    )
    average = jnp.mean(carried, axis=1, keepdims=True)
    centred = carried - average
    variance = jnp.mean(centred * centred, axis=1, keepdims=True)
    normed = (centred * lax.rsqrt(variance + EPS) * norm_gain + norm_bias).astype(jnp.bfloat16)
    halves = jnp.dot(normed, gather(glu_proj), preferred_element_type=jnp.float32)
    feature_count = halves.shape[1] // 2
    gated_rows = (halves[:, :feature_count] * jax.nn.sigmoid(halves[:, feature_count:])).astype(
        jnp.bfloat16
    )
    swished = convolve(gated_rows, segment, conv_taps, batch_scale, batch_shift)
    lowered = jnp.dot(swished, gather(down_proj), preferred_element_type=jnp.float32)
    centre_segment = segment[HALO : HALO + slab_rows]
    own_carried = carried[HALO : HALO + slab_rows]
    return jnp.where((centre_segment >= 0)[:, None], own_carried + lowered, 0.0).astype(
        jnp.bfloat16
    )


def solution(mesh):
    in_specs = (
        P("dp", "mp", None),
        P("dp", "mp", None),
        P("dp", "mp", None),
        P("dp", "mp", None),
        P(),
        P(),
        P(None, "mp"),
        P(),
        P(),
        P(None, "mp"),
        P(),
        P(),
        P(),
        P(None, "mp"),
    )
    out_specs = P(("dp", "mp"), None)
    return jax.shard_map(
        on_device, mesh=mesh, in_specs=in_specs, out_specs=out_specs, check_vma=False
    )
```

profile of v0, /device:TPU:0, one launch (start us, length us, event | category | flops | bytes accessed | tf_op | source)
XLA Modules:
  0.0 360.8 jit_solution(13630915954185177964)
XLA Ops:
  8.0 4.5 %reshape_reshape.3.rows_ref = bf16[4096,192]{1,0:T(8,128)(2,1)} reshape(bf16[1024,1,768]{2,0,1:T(8,128)(2,1)} %param.17) | data formatting | bytes 3145728 | tf_op jit(solution)/shard_map/reshape;reshape | solution.py:324
  14.1 3.8 %shard_map.136 = bf16[16,256,192]{2,1,0:T(8,128)(2,1)} custom-call(s32[16]{0:T(128)} %get-tuple-element.6.start_ref, bf16[4096,192]{1,0:T(8,128)(2,1)} %reshape_reshape.3.rows_ref), custom_call_target="tpu_custom_call" | custom-call | tf_op jit(solution)/shard_map/pallas_call | solution.py:144
  17.9 4.0 %copy.23 = bf16[16,256,192]{1,2,0:T(8,128)(2,1)} copy(bf16[16,256,192]{2,1,0:T(8,128)(2,1)} %shard_map.136) | data formatting | bytes 3145728 | tf_op jit(solution)/shard_map/pallas_call | solution.py:144
  21.8 4.3 %all-to-all-start = ((bf16[16,256,192]{1,2,0:T(8,128)(2,1)}), bf16[16,256,192]{1,2,0:T(8,128)(2,1)S(1)}, u32[]{:S(2)}, u32[]{:S(2)}) async-start(bf16[16,256,192]{1,2,0:T(8,128)(2,1)} %copy.23), calls=%async_computation | async-start | bytes 3145728 | tf_op jit(solution)/shard_map/all_to_all | solution.py:328
  27.3 3.2 copy_bitcast_fusion
  30.5 19.1 %shard_map.138 = bf16[16,256,128]{2,1,0:T(8,128)(2,1)} custom-call(s32[16]{0:T(128)} %get-tuple-element.6.start_ref, s32[16]{0:T(128)} %get-tuple-element.5.span_ref, bf16[2048,256]{1,0:T(8,128)(2,1)} %bitcast.46, bf16[2048,256]{1,0:T(8,128)(2,1)} %get-tuple-element.23.k_ref, bf16[2048,256]{1,0:T(8,128)(2,1)} %get-tuple-element.22.v_ref), custom_call_target="tpu_custom_call" | custom-call | flops 1073741824 | bytes 4194304 | tf_op jit(solution)/shard_map/pallas_call | solution.py:98
  49.6 3.6 all-to-all-start.2
  53.9 2.5 copy.24.slots_ref
  56.4 3.9 %shard_map.137 = bf16[8,544,192]{2,1,0:T(8,128)(2,1)} custom-call(s32[17]{0:T(128)} %select_reduce_fusion.1.after_ref, bf16[16,256,192]{2,1,0:T(8,128)(2,1)} %copy.24.slots_ref), custom_call_target="tpu_custom_call" | custom-call | tf_op jit(solution)/shard_map/pallas_call | solution.py:190
  60.3 4.1 %copy.25 = bf16[8,544,192]{1,2,0:T(8,128)(2,1)} copy(bf16[8,544,192]{2,1,0:T(8,128)(2,1)} %shard_map.137) | data formatting | bytes 3342336 | tf_op jit(solution)/shard_map/pallas_call | solution.py:190
  64.4 3.2 all-to-all-done.2.slots_ref
  67.6 6.5 %all-to-all-start.1 = ((bf16[8,544,192]{1,2,0:T(8,128)(2,1)}), bf16[8,544,192]{1,2,0:T(8,128)(2,1)S(1)}, u32[]{:S(2)}, u32[]{:S(2)}) async-start(bf16[8,544,192]{1,2,0:T(8,128)(2,1)} %copy.25), calls=%async_computation.1 | async-start | bytes 3932160 | tf_op jit(solution)/shard_map/all_to_all | solution.py:328
  74.9 2.7 shard_map.139
  77.5 77.1 %all-to-all-done.1 = bf16[8,544,192]{1,2,0:T(8,128)(2,1)S(1)} async-done(((bf16[8,544,192]{1,2,0:T(8,128)(2,1)}), bf16[8,544,192]{1,2,0:T(8,128)(2,1)S(1)}, u32[]{:S(2)}, u32[]{:S(2)}) %all-to-all-start.1) | async-done | bytes 1671200 | tf_op jit(solution)/shard_map/all_to_all | solution.py:328
  154.6 6.2 %all-to-all-start.3 = ((bf16[8,544,128]{2,1,0:T(8,128)(2,1)}), bf16[8,544,128]{2,1,0:T(8,128)(2,1)}, u32[]{:S(2)}, u32[]{:S(2)}) async-start(bf16[8,544,128]{2,1,0:T(8,128)(2,1)} %shard_map.139), calls=%async_computation.3 | async-start | bytes 2228224 | tf_op jit(solution)/shard_map/all_to_all | solution.py:328
  163.8 2.1 convert_element_type.37
  166.0 3.5 copy.27
  169.5 56.5 %all-to-all-done.3 = bf16[8,544,128]{2,1,0:T(8,128)(2,1)} async-done(((bf16[8,544,128]{2,1,0:T(8,128)(2,1)}), bf16[8,544,128]{2,1,0:T(8,128)(2,1)}, u32[]{:S(2)}, u32[]{:S(2)}) %all-to-all-start.3) | async-done | bytes 1114144 | tf_op jit(solution)/shard_map/all_to_all | solution.py:328
  225.9 4.3 %fusion.20 = (f32[544]{0:T(1024)S(1)}, f32[544,1536]{1,0:T(8,128)S(1)}) fusion(f32[544,1536]{1,0:T(8,128)S(1)} %copy.27, bf16[1024,1536]{0,1:T(8,128)(2,1)} %all-gather.4.cloned.1.call-done, bf16[8,544,128]{2,1,0:T(8,128)(2,1)} %all-to-all-done.3), kind=kOutput, calls=%fused_computation.61 | convolution fusion | flops 1712946688 | bytes 10946688 | tf_op jit(solution)/shard_map/dot_general | solution.py:340
  232.4 34.0 %all-gather.6.cloned.1.call-done = bf16[1536,3072]{1,0:T(8,128)(2,1)} async-done(((bf16[1536,384]{1,0:T(8,128)(2,1)}), bf16[1536,3072]{1,0:T(8,128)(2,1)}) %all-gather.6.cloned.1.call-update) | async-done | bytes 9437200 | tf_op jit(solution)/shard_map/all_gather | solution.py:338
  266.4 9.1 %fusion.7 = f32[544,3072]{1,0:T(8,128)S(1)} fusion(bf16[1536,3072]{1,0:T(8,128)(2,1)} %all-gather.6.cloned.1.call-done, f32[544,1536]{1,0:T(8,128)} %copy-done.1, f32[1536]{0:T(1024)S(1)} %copy-done.9, f32[1536]{0:T(1024)S(1)} %copy-done.10, f32[544]{0:T(1024)S(1)} %add_rsqrt_fusion, f32[544]{0:T(1024)S(1)} %broadcast_multiply_fusion), kind=kOutput, calls=%fused_computation.12 | convolution fusion | flops 5138006016 | bytes 19480832 | tf_op jit(solution)/shard_map/dot_general | solution.py:347
  278.4 14.8 %shard_map.140 = bf16[512,1536]{1,0:T(8,128)(2,1)} custom-call(s32[8]{0:T(128)} %convert_element_type.32.uniform_ref, bf16[544,1536]{1,0:T(8,128)(2,1)} %fusion.4.gated_ref, s32[544,128]{1,0:T(8,128)} %broadcast_in_dim.113.segment_ref, f32[31,1536]{1,0:T(8,128)} %taps_ref.1, f32[1,1536]{1,0:T(1,128)} %broadcast_in_dim.114.scale_ref, ...), custom_call_target="tpu_custom_call" | custom-call | flops 48758784 | bytes 3145728 | tf_op jit(solution)/shard_map/pallas_call | solution.py:245
  293.2 54.5 %all-gather.8.cloned.1.call-done = bf16[1536,1536]{0,1:T(8,128)(2,1)} async-done(((bf16[1536,192]{0,1:T(8,128)(2,1)}), bf16[1536,1536]{0,1:T(8,128)(2,1)}) %all-gather.8.cloned.1.call-update) | async-done | bytes 4718608 | tf_op jit(solution)/shard_map/all_gather | solution.py:338
  347.7 6.6 %fusion.6 = bf16[512,1536]{1,0:T(8,128)(2,1)} fusion(bf16[512,1536]{1,0:T(8,128)(2,1)} %shard_map.140, bf16[1536,1536]{0,1:T(8,128)(2,1)} %all-gather.8.cloned.1.call-done, f32[544,1536]{1,0:T(8,128)S(1)} %copy-done.2, pred[512]{0:T(512)(128)(4,1)S(1)} %slice_compare_fusion), kind=kOutput, calls=%fused_computation.11 | convolution fusion | flops 2418278400 | bytes 11010560 | tf_op jit(solution)/shard_map/dot_general | solution.py:353
  (55 shorter events, 13.6 us)
Async XLA Ops:
  6.5 6.0 %copy-start.6 = (s32[64]{0:T(128)S(1)}, s32[64]{0:T(128)}, u32[]{:S(2)}) copy-start(s32[64]{0:T(128)} %param.18) | copy-start | bytes 772
  6.5 6.0 %copy-start.8 = (s32[64]{0:T(128)S(1)}, s32[64]{0:T(128)}, u32[]{:S(2)}) copy-start(s32[64]{0:T(128)} %param.19) | copy-start | bytes 772
  6.5 219.4 %all-gather.4.cloned.1.call-start = ((), (), s32[]{:S(2)}) async-start(), calls=%async_computation.4 | async-start | bytes 3538944 | tf_op jit(solution)/shard_map/all_gather | solution.py:338
  7.3 259.1 %all-gather.6.cloned.1.call-start = ((), (), s32[]{:S(2)}) async-start(), calls=%async_computation.5 | async-start | bytes 10616832 | tf_op jit(solution)/shard_map/all_gather | solution.py:338
  17.9 8.3 %copy-start.3 = (bf16[2048,2,128]{2,1,0:T(2,128)(2,1)S(1)}, bf16[2048,2,128]{2,1,0:T(2,128)(2,1)}, u32[]{:S(2)}) copy-start(bf16[2048,2,128]{2,1,0:T(2,128)(2,1)} %param.14) | copy-start | bytes 3145732
  21.8 27.8 %all-to-all-start = ((bf16[16,256,192]{1,2,0:T(8,128)(2,1)}), bf16[16,256,192]{1,2,0:T(8,128)(2,1)S(1)}, u32[]{:S(2)}, u32[]{:S(2)}) async-start(bf16[16,256,192]{1,2,0:T(8,128)(2,1)} %copy.23), calls=%async_computation | async-start | bytes 3145728 | tf_op jit(solution)/shard_map/all_to_all | solution.py:328
  49.6 18.0 %all-to-all-start.2 = ((bf16[16,256,128]{2,1,0:T(8,128)(2,1)}), bf16[16,256,128]{2,1,0:T(8,128)(2,1)S(1)}, u32[]{:S(2)}, u32[]{:S(2)}) async-start(bf16[16,256,128]{2,1,0:T(8,128)(2,1)} %shard_map.138), calls=%async_computation.2 | async-start | bytes 2097152 | tf_op jit(solution)/shard_map/all_to_all | solution.py:328
  67.6 7.2 %copy-start = (bf16[16,256,128]{2,1,0:T(8,128)(2,1)}, bf16[16,256,128]{2,1,0:T(8,128)(2,1)S(1)}, u32[]{:S(2)}) copy-start(bf16[16,256,128]{2,1,0:T(8,128)(2,1)S(1)} %all-to-all-done.2.slots_ref) | copy-start | bytes 3145732
  67.6 87.0 %all-to-all-start.1 = ((bf16[8,544,192]{1,2,0:T(8,128)(2,1)}), bf16[8,544,192]{1,2,0:T(8,128)(2,1)S(1)}, u32[]{:S(2)}, u32[]{:S(2)}) async-start(bf16[8,544,192]{1,2,0:T(8,128)(2,1)} %copy.25), calls=%async_computation.1 | async-start | bytes 3932160 | tf_op jit(solution)/shard_map/all_to_all | solution.py:328
  74.1 86.8 %copy-start.7 = (s32[17]{0:T(128)S(1)}, s32[17]{0:T(128)}, u32[]{:S(2)}) copy-start(s32[17]{0:T(128)} %select_reduce_fusion.1.after_ref) | copy-start | bytes 208
  74.1 88.5 %copy-start.4 = (f32[1536]{0:T(1024)S(1)}, f32[1536]{0:T(1024)}, u32[]{:S(2)}) copy-start(f32[1536]{0:T(1024)} %param.25) | copy-start | bytes 18436
  74.1 89.1 %copy-start.5 = (f32[1536]{0:T(1024)S(1)}, f32[1536]{0:T(1024)}, u32[]{:S(2)}) copy-start(f32[1536]{0:T(1024)} %param.26) | copy-start | bytes 18436
  74.1 273.6 %all-gather.8.cloned.1.call-start = ((), (), s32[]{:S(2)}) async-start(), calls=%async_computation.6 | async-start | bytes 5308416 | tf_op jit(solution)/shard_map/all_gather | solution.py:338
  154.6 71.3 %all-to-all-start.3 = ((bf16[8,544,128]{2,1,0:T(8,128)(2,1)}), bf16[8,544,128]{2,1,0:T(8,128)(2,1)}, u32[]{:S(2)}, u32[]{:S(2)}) async-start(bf16[8,544,128]{2,1,0:T(8,128)(2,1)} %shard_map.139), calls=%async_computation.3 | async-start | bytes 2228224 | tf_op jit(solution)/shard_map/all_to_all | solution.py:328
  230.3 1.7 copy-start.1
  230.3 36.1 %copy-start.9 = (f32[1536]{0:T(1024)S(1)}, f32[1536]{0:T(1024)}, u32[]{:S(2)}) copy-start(f32[1536]{0:T(1024)} %param.22) | copy-start | bytes 18436
  230.3 36.1 %copy-start.10 = (f32[1536]{0:T(1024)S(1)}, f32[1536]{0:T(1024)}, u32[]{:S(2)}) copy-start(f32[1536]{0:T(1024)} %param.21) | copy-start | bytes 18436
  277.6 70.1 %copy-start.2 = (f32[544,1536]{1,0:T(8,128)S(1)}, f32[544,1536]{1,0:T(8,128)}, u32[]{:S(2)}) copy-start(f32[544,1536]{1,0:T(8,128)} %copy-done.1) | copy-start | bytes 10027012
Sparse Core Ops, SparseCore 0:
  9.5 62.6 all-gather.3
  74.3 192.0 all-gather.5
  268.6 79.0 all-gather.7
where the time goes:
time: 362 us; the launch traced here: 361 us
  waiting for transfers between devices  227 us (63%)
  Pallas kernels  44.3 us (12%)
  local copies, waits for them, and re-layouts  26.8 us (7%)
  starting transfers between devices  20.7 us (6%)
  matrix products  20 us (6%)
  between operations  13.2 us (4%)
  other arithmetic  8.43 us (2%)
    all_to_all x4, waiting for transfers between devices, swap(): return lax.all_to_all(array, axis, split_axis=0, concat_axis=0, tiled=True)  137 us
    all_gather x3, waiting for transfers between devices, gather(): return lax.all_gather(weights, 'mp', axis=1, tiled=True)  88.4 us
    all_to_all x4, starting transfers between devices, swap(): return lax.all_to_all(array, axis, split_axis=0, concat_axis=0, tiled=True)  20.6 us
    pallas_call x1, Pallas kernels, attend(): pl.pallas_call(functools.partial(attention_kernel, heads), out_shape=jax....  19.1 us
    pallas_call x1, Pallas kernels, convolve(): pl.pallas_call(conv_kernel, grid=(width // LANES,), out_shape=jax.ShapeDt...  14.8 us
    dot_general x1, matrix products, on_device(): jnp.dot(normed, gather(glu_proj), preferred_element_type=jnp.float32)  9.05 us
  transfers between devices with their start and end apart: 7, of which 5 were waited for; matrix products, arithmetic and copies ran while one was open for 13% of the time, Pallas kernels for 12%

commit v1 on v0

--- a/solution.py
+++ b/solution.py
@@ -85,7 +85,7 @@
             weights = (exponentials / denominator).astype(jnp.bfloat16)
             blended = jnp.dot(weights, values, preferred_element_type=jnp.float32)
             result = blended if head == 0 else jnp.where(head_lane == head, blended, result)
-        out_ref[slot] = result[:, : heads * HD].astype(jnp.bfloat16)
+        out_ref[slot] = result.astype(jnp.bfloat16)
         return carry
 
     lax.fori_loop(0, start_ref.shape[0], slot_body, 0)
@@ -97,7 +97,7 @@
     flat = [a.reshape(pairs, heads * LANES) for a in (query_rows, key_rows, value_rows)]
     return pl.pallas_call(
         functools.partial(attention_kernel, heads),
-        out_shape=jax.ShapeDtypeStruct((slots, MAXLEN, heads * HD), jnp.bfloat16),
+        out_shape=jax.ShapeDtypeStruct((slots, MAXLEN, LANES), jnp.bfloat16),
         in_specs=[smem_spec()] * 2 + [whole_spec()] * 3,
         out_specs=whole_spec(),
         scratch_shapes=[pltpu.VMEM((2 * pairs + MAXLEN, LANES), jnp.float32)] * 3,
@@ -114,6 +114,29 @@
     return [(first, min(LANES, width - first)) for first in range(0, width, LANES)]
 
 
+def pairable(width):
+    return width == LANES + LANES // 2
+
+
+def join_pair(one, two):
+    half = LANES // 2
+    low = lax.broadcasted_iota(jnp.int32, one[0].shape, 1) < half
+    turned = pltpu.roll(two[0], half, 1)
+    return (
+        one[0],
+        jnp.where(low, one[1], turned),
+        jnp.where(low, turned, pltpu.roll(two[1], half, 1)),
+    )
+
+
+def split_pair(tiles):
+    half = LANES // 2
+    low = lax.broadcasted_iota(jnp.int32, tiles[0].shape, 1) < half
+    middle = pltpu.roll(tiles[1], half, 1)
+    last = pltpu.roll(tiles[2], half, 1)
+    return (tiles[0], tiles[1]), (jnp.where(low, middle, last), last)
+
+
 def slots_kernel(start_ref, rows_ref, out_ref, *held):
     count, width = rows_ref.shape
     for (first, size), rows in zip(lane_tiles(width), held):
@@ -129,73 +152,130 @@
         rows[pl.ds(count, MAXLEN), :] = jnp.zeros((MAXLEN, LANES), jnp.float32)
 
     def slot_body(slot, carry):
-        start = start_ref[slot]
-        for (first, size), rows in zip(lane_tiles(width), held):
-            taken = rows[pl.ds(start, MAXLEN), :]
-            out_ref[slot, :, first : first + size] = taken[:, :size].astype(jnp.bfloat16)
-        return carry
-
-    lax.fori_loop(0, start_ref.shape[0], slot_body, 0)
+        if pairable(width):
+            pair = [
+                [rows[pl.ds(start_ref[2 * slot + side], MAXLEN), :] for rows in held]
+                for side in range(2)
+            ]
+            tiles = join_pair(*pair)
+        else:
+            tiles = [rows[pl.ds(start_ref[slot], MAXLEN), :] for rows in held]
+        for index, tile in enumerate(tiles):
+            out_ref[slot, :, index * LANES : (index + 1) * LANES] = tile.astype(jnp.bfloat16)
+        return carry
+
+    lax.fori_loop(0, out_ref.shape[0], slot_body, 0)
 
 
 def into_slots(start, rows):
     count, width = rows.shape
     slots = start.shape[0]
+    tiles = len(lane_tiles(width))
+    shape = (slots, MAXLEN, tiles * LANES)
+    if pairable(width):
+        shape = (slots // 2, MAXLEN, 2 * width)
     return pl.pallas_call(
         slots_kernel,
-        out_shape=jax.ShapeDtypeStruct((slots, MAXLEN, width), jnp.bfloat16),
+        out_shape=jax.ShapeDtypeStruct(shape, jnp.bfloat16),
         in_specs=[smem_spec(), whole_spec()],
         out_specs=whole_spec(),
-        scratch_shapes=[pltpu.VMEM((count + MAXLEN, LANES), jnp.float32)] * len(lane_tiles(width)),
+        scratch_shapes=[pltpu.VMEM((count + MAXLEN, LANES), jnp.float32)] * tiles,
         compiler_params=params(),
     )(start, rows)
 
 
-def place_kernel(after_ref, slots_ref, out_ref, *held):
-    slots, _, width = slots_ref.shape
-    slabs, tall, _ = out_ref.shape
+def place_kernel(paired, after_ref, x_ref, context_ref, out_ref, context_rows, *x_rows):
+    slots = context_ref.shape[0]
+    slabs = out_ref.shape[0]
+    tall = out_ref.shape[1] * (2 if paired else 1)
     slab_rows = tall - 2 * HALO
-    total_rows = held[0].shape[0]
+    total_rows = context_rows.shape[0]
+    held = (context_rows,) + x_rows
     zeros = jnp.zeros((MAXLEN, LANES), jnp.float32)
-    for (first, size), rows in zip(lane_tiles(width), held):
+    for rows in held:
         rows[pl.ds(0, HALO), :] = jnp.zeros((HALO, LANES), jnp.float32)
 
-        def put(slot, carry):
-            rows[pl.ds(HALO + after_ref[slot], MAXLEN), 0:size] = slots_ref[
-                slot, :, first : first + size
-            ].astype(jnp.float32)
-            return carry
-
-        lax.fori_loop(0, slots, put, 0)
-        live = after_ref[slots]
-
-        def clear(step, carry):
-            at = jnp.minimum(HALO + live + step * MAXLEN, total_rows - MAXLEN)
+    def load(ref, slot, tile):
+        return ref[slot, :, tile * LANES : (tile + 1) * LANES].astype(jnp.float32)
+
+    def put(step, carry):
+        if paired:
+            sides = split_pair([load(x_ref, step, tile) for tile in range(3)])
+            for side in range(2):
+                slot = 2 * step + side
+                where = pl.ds(HALO + after_ref[slot], MAXLEN)
+                for rows, piece in zip(x_rows, sides[side]):
+                    rows[where, :] = piece
+                context_rows[where, :] = load(context_ref, slot, 0)
+        else:
+            where = pl.ds(HALO + after_ref[step], MAXLEN)
+            for tile, rows in enumerate(x_rows):
+                rows[where, :] = load(x_ref, step, tile)
+            context_rows[where, :] = load(context_ref, step, 0)
+        return carry
+
+    lax.fori_loop(0, x_ref.shape[0], put, 0)
+    live = after_ref[slots]
+
+    def clear(step, carry):
+        at = jnp.minimum(HALO + live + step * MAXLEN, total_rows - MAXLEN)
+        for rows in held:
             rows[pl.ds(at, MAXLEN), :] = zeros
-            return carry
-
-        lax.fori_loop(0, (total_rows - HALO - live + MAXLEN - 1) // MAXLEN, clear, 0)
-
-        def emit(slab, carry):
-            at = pl.multiple_of(slab * slab_rows, slab_rows)
-            taken = rows[pl.ds(at, tall), :]
-            out_ref[slab, :, first : first + size] = taken[:, :size].astype(jnp.bfloat16)
-            return carry
-
-        lax.fori_loop(0, slabs, emit, 0)
-
-
-def place(after, slots, slabs, slab_rows):
-    count, _, width = slots.shape
+        return carry
+
+    lax.fori_loop(0, (total_rows - HALO - live + MAXLEN - 1) // MAXLEN, clear, 0)
+
+    def emit(slab, carry):
+        at = pl.multiple_of(slab * slab_rows, slab_rows)
+        if paired:
+            half = tall // 2
+            one = pl.ds(at, half)
+            two = pl.ds(pl.multiple_of(at + half, 8), half)
+            tiles = join_pair([rows[one, :] for rows in x_rows], [rows[two, :] for rows in x_rows])
+            tiles = tiles + (context_rows[one, :], context_rows[two, :])
+        else:
+            tiles = [rows[pl.ds(at, tall), :] for rows in x_rows + (context_rows,)]
+        for index, tile in enumerate(tiles):
+            out_ref[slab, :, index * LANES : (index + 1) * LANES] = tile.astype(jnp.bfloat16)
+        return carry
+
+    lax.fori_loop(0, slabs, emit, 0)
+
+
+def place(after, x_slots, context_slots, slabs, slab_rows, features):
+    count = context_slots.shape[0]
+    paired = pairable(features)
+    tiles = len(lane_tiles(features))
+    tall = slab_rows + 2 * HALO
+    shape = (slabs, tall, (tiles + 1) * LANES)
+    if paired:
+        shape = (slabs, tall // 2, 2 * features + 2 * LANES)
     return pl.pallas_call(
-        place_kernel,
-        out_shape=jax.ShapeDtypeStruct((slabs, slab_rows + 2 * HALO, width), jnp.bfloat16),
-        in_specs=[smem_spec(), whole_spec()],
+        functools.partial(place_kernel, paired),
+        out_shape=jax.ShapeDtypeStruct(shape, jnp.bfloat16),
+        in_specs=[smem_spec(), whole_spec(), whole_spec()],
         out_specs=whole_spec(),
         scratch_shapes=[pltpu.VMEM((count * MAXLEN + HALO + MAXLEN, LANES), jnp.float32)]
-        * len(lane_tiles(width)),
+        * (tiles + 1),
         compiler_params=params(),
-    )(after, slots)
+    )(after, x_slots, context_slots)
+
+
+def unplace(moved, features, context_width):
+    slabs, rows, _ = moved.shape
+    if not pairable(features):
+        first = len(lane_tiles(features)) * LANES
+        x = moved[:, :, :features].transpose(1, 0, 2).reshape(rows, -1)
+        context = moved[:, :, first : first + context_width]
+        return x, context.transpose(1, 0, 2).reshape(rows, -1)
+
+    def sides(part, width):
+        return part.reshape(slabs, rows, 2, width).transpose(2, 1, 0, 3).reshape(2 * rows, -1)
+
+    return (
+        sides(moved[:, :, : 2 * features], features),
+        sides(moved[:, :, 2 * features :], context_width),
+    )
 
 
 def conv_kernel(
@@ -308,7 +388,6 @@
     leaving = (source[None, :] == data_group) & ((assignment * PIECES + rank)[None, :] == slot)
     start = jnp.sum(jnp.where(leaving, before[None, :], 0), axis=1)
     span = jnp.sum(jnp.where(leaving, lengths[None, :], 0), axis=1)
-    coming = (assignment[None, :] == data_group) & ((source * PIECES + rank)[None, :] == slot)
     coming_earlier = (assignment[None, :] == data_group) & (
         (source * PIECES + rank)[None, :] < jnp.arange(slots + 1, dtype=jnp.int32)[:, None]
     )
@@ -327,30 +406,41 @@
     def swap(array, axis):
         return lax.all_to_all(array, axis, split_axis=0, concat_axis=0, tiled=True)
 
-    def carry_over(array):
-        placed = place(after, swap(array, "dp"), slabs, slab_rows)
-        return swap(placed, "mp").transpose(1, 0, 2).reshape(slab_rows + 2 * HALO, -1)
-
-    carried_slab = carry_over(into_slots(start, residual_rows))
-    context_slab = carry_over(attend(start, span, query_rows, key_rows, value_rows))
+    x_slots = swap(into_slots(start, residual_rows), "dp")
+    context_slots = swap(attend(start, span, query_rows, key_rows, value_rows), "dp")
+    moved = swap(place(after, x_slots, context_slots, slabs, slab_rows, features), "mp")
+    carried_slab, context_slab = unplace(moved, features, query_rows.shape[1] * HD)
+
+    core = data_group % 2
+    partners = [(group, group + 1 - 2 * (group % 2)) for group in range(groups)]
 
     def gather(weights):
-        return lax.all_gather(weights, "mp", axis=1, tiled=True)
-
-    carried = carried_slab.astype(jnp.float32) + jnp.dot(
-        context_slab, gather(out_proj), preferred_element_type=jnp.float32
-    )
+        half = weights.shape[0] // 2
+        own = lax.dynamic_slice_in_dim(weights, core * half, half, 0)
+        own = lax.all_gather(own, "mp", axis=1, tiled=True)
+        return own, lax.ppermute(own, "dp", partners)
+
+    def project(rows, halves_of):
+        own, other = halves_of
+        half = rows.shape[1] // 2
+        low, high = rows[:, :half], rows[:, half:]
+        return jnp.dot(
+            jnp.where(core == 0, low, high), own, preferred_element_type=jnp.float32
+        ) + jnp.dot(jnp.where(core == 0, high, low), other, preferred_element_type=jnp.float32)
+
+    out_halves, glu_halves, down_halves = gather(out_proj), gather(glu_proj), gather(down_proj)
+    carried = carried_slab.astype(jnp.float32) + project(context_slab, out_halves)
     average = jnp.mean(carried, axis=1, keepdims=True)
     centred = carried - average
     variance = jnp.mean(centred * centred, axis=1, keepdims=True)
     normed = (centred * lax.rsqrt(variance + EPS) * norm_gain + norm_bias).astype(jnp.bfloat16)
-    halves = jnp.dot(normed, gather(glu_proj), preferred_element_type=jnp.float32)
+    halves = project(normed, glu_halves)
     feature_count = halves.shape[1] // 2
     gated_rows = (halves[:, :feature_count] * jax.nn.sigmoid(halves[:, feature_count:])).astype(
         jnp.bfloat16
     )
     swished = convolve(gated_rows, segment, conv_taps, batch_scale, batch_shift)
-    lowered = jnp.dot(swished, gather(down_proj), preferred_element_type=jnp.float32)
+    lowered = project(swished, down_halves)
     centre_segment = segment[HALO : HALO + slab_rows]
     own_carried = carried[HALO : HALO + slab_rows]
     return jnp.where((centre_segment >= 0)[:, None], own_carried + lowered, 0.0).astype(

time: 362 us -> 291 us (0.80)
  waiting for transfers between devices: 227 us -> 150 us
  local copies, waits for them, and re-layouts: 26.8 us -> 35.8 us
  starting transfers between devices: 20.7 us -> 14.7 us
    all_to_all x4 -> x3, waiting for transfers between devices: 137 us -> 26.7 us  [swap(): return lax.all_to_all(array, axis, split_axis=0, concat_axis=0, tiled=True)]
    all_gather x3, waiting for transfers between devices: 88.4 us -> 123 us  [gather(): own = lax.all_gather(own, 'mp', axis=1, tiled=True)]
    convert_element_type x1 -> x3, local copies, waits for them, and re-layouts: 3.47 us -> 18.8 us  [on_device(): carried_slab.astype(jnp.float32) + project(context_slab, out_halves)]
    pallas_call x2 -> x0, local copies, waits for them, and re-layouts: 8.04 us -> none  [the longest x1 4.08 us: place(): pl.pallas_call(place_kernel, out_shape=jax.ShapeDtypeStruct((slabs, slab_...]
    all_to_all x4 -> x3, starting transfers between devices: 20.6 us -> 14.6 us  [swap(): return lax.all_to_all(array, axis, split_axis=0, concat_axis=0, tiled=True)]
    dot_general x3 -> x6, matrix products: 20 us -> 21 us  [the longest x3 11.9 us: project(): jnp.dot(jnp.where(core == 0, high, low), other, preferred_element_type=jn...]
    pallas_call x3 -> x2, Pallas kernels: 10.4 us -> 9.36 us  [the longest x1 5.32 us: place(): pl.pallas_call(functools.partial(place_kernel, paired), out_shape=jax.Sha...]
  transfers between devices with their start and end apart: 7 -> 9, of which waited for: 5 -> 5; matrix products, arithmetic and copies ran while one was open for 13% -> 21% of each run, Pallas kernels for 12% -> 15%
where the time goes in v1:
time: 291 us; the launch traced here: 289 us
  waiting for transfers between devices  150 us (52%)
  Pallas kernels  43.1 us (15%)
  local copies, waits for them, and re-layouts  35.8 us (12%)
  matrix products  21 us (7%)
  starting transfers between devices  14.7 us (5%)
  between operations  13.4 us (5%)
  other arithmetic  11.7 us (4%)
    all_gather x3, waiting for transfers between devices, gather(): own = lax.all_gather(own, 'mp', axis=1, tiled=True)  123 us
    all_to_all x3, waiting for transfers between devices, swap(): return lax.all_to_all(array, axis, split_axis=0, concat_axis=0, tiled=True)  26.7 us
    pallas_call x1, Pallas kernels, attend(): pl.pallas_call(functools.partial(attention_kernel, heads), out_shape=jax....  19.2 us
    convert_element_type x3, local copies, waits for them, and re-layouts, on_device(): carried_slab.astype(jnp.float32) + project(context_slab, out_halves)  18.8 us
    all_to_all x3, starting transfers between devices, swap(): return lax.all_to_all(array, axis, split_axis=0, concat_axis=0, tiled=True)  14.6 us
    pallas_call x1, Pallas kernels, convolve(): pl.pallas_call(conv_kernel, grid=(width // LANES,), out_shape=jax.ShapeDt...  14.6 us
    dot_general x3, matrix products, project(): jnp.dot(jnp.where(core == 0, high, low), other, preferred_element_type=jn...  11.9 us
    dot_general x3, matrix products, project(): jnp.dot(jnp.where(core == 0, low, high), own, preferred_element_type=jnp....  9.11 us
  transfers between devices with their start and end apart: 9, of which 5 were waited for; matrix products, arithmetic and copies ran while one was open for 21% of the time, Pallas kernels for 15%

profile of v1, /device:TPU:0, one launch (start us, length us, event | category | flops | bytes accessed | tf_op | source)
XLA Modules:
  0.0 289.3 jit_solution(12638242618857034756)
XLA Ops:
  13.9 1.7 copy_bitcast_fusion.1
  16.3 19.2 %shard_map.137 = bf16[16,256,128]{2,1,0:T(8,128)(2,1)} custom-call(s32[16]{0:T(128)} %get-tuple-element.6.start_ref, s32[16]{0:T(128)} %get-tuple-element.5.span_ref, bf16[2048,256]{1,0:T(8,128)(2,1)} %bitcast.45, bf16[2048,256]{1,0:T(8,128)(2,1)} %get-tuple-element.23.k_ref, bf16[2048,256]{1,0:T(8,128)(2,1)} %get-tuple-element.22.v_ref), custom_call_target="tpu_custom_call" | custom-call | flops 1073741824 | bytes 4194304 | tf_op jit(solution)/shard_map/pallas_call | solution.py:98
  35.5 4.4 %all-to-all-start.1 = ((bf16[16,256,128]{2,1,0:T(8,128)(2,1)}), bf16[16,256,128]{2,1,0:T(8,128)(2,1)S(1)}, u32[]{:S(2)}, u32[]{:S(2)}) async-start(bf16[16,256,128]{2,1,0:T(8,128)(2,1)} %shard_map.137), calls=%async_computation.1 | async-start | bytes 2097152 | tf_op jit(solution)/shard_map/all_to_all | solution.py:407
  39.9 3.0 %reshape_reshape.3.rows_ref = bf16[4096,192]{1,0:T(8,128)(2,1)} reshape(bf16[1024,1,768]{2,0,1:T(8,128)(2,1)S(1)} %copy-done.8) | data formatting | bytes 3145728 | tf_op jit(solution)/shard_map/reshape;reshape | solution.py:403
  42.8 4.0 %shard_map.136 = bf16[8,256,384]{2,1,0:T(8,128)(2,1)} custom-call(s32[16]{0:T(128)} %get-tuple-element.6.start_ref, bf16[4096,192]{1,0:T(8,128)(2,1)} %reshape_reshape.3.rows_ref), custom_call_target="tpu_custom_call" | custom-call | tf_op jit(solution)/shard_map/pallas_call | solution.py:177
  46.9 7.4 %all-to-all-done.1.context_ref = bf16[16,256,128]{2,1,0:T(8,128)(2,1)S(1)} async-done(((bf16[16,256,128]{2,1,0:T(8,128)(2,1)}), bf16[16,256,128]{2,1,0:T(8,128)(2,1)S(1)}, u32[]{:S(2)}, u32[]{:S(2)}) %all-to-all-start.1) | async-done | bytes 1048608 | tf_op jit(solution)/shard_map/all_to_all | solution.py:407
  54.3 3.6 %all-to-all-start = ((bf16[8,256,384]{2,1,0:T(8,128)(2,1)}), bf16[8,256,384]{2,1,0:T(8,128)(2,1)S(1)}, u32[]{:S(2)}, u32[]{:S(2)}) async-start(bf16[8,256,384]{2,1,0:T(8,128)(2,1)} %shard_map.136), calls=%async_computation | async-start | bytes 3145728 | tf_op jit(solution)/shard_map/all_to_all | solution.py:407
  58.6 19.3 %all-to-all-done.x_ref = bf16[8,256,384]{2,1,0:T(8,128)(2,1)S(1)} async-done(((bf16[8,256,384]{2,1,0:T(8,128)(2,1)}), bf16[8,256,384]{2,1,0:T(8,128)(2,1)S(1)}, u32[]{:S(2)}, u32[]{:S(2)}) %all-to-all-start) | async-done | bytes 1572896 | tf_op jit(solution)/shard_map/all_to_all | solution.py:407
  79.1 5.3 %shard_map.138 = bf16[8,272,640]{2,1,0:T(8,128)(2,1)} custom-call(s32[17]{0:T(128)} %select_reduce_fusion.1.after_ref, bf16[8,256,384]{2,1,0:T(8,128)(2,1)} %copy-done.5, bf16[16,256,128]{2,1,0:T(8,128)(2,1)} %copy-done.6), custom_call_target="tpu_custom_call" | custom-call | tf_op jit(solution)/shard_map/pallas_call | solution.py:253
  84.4 6.7 %all-to-all-start.2 = ((bf16[8,272,640]{2,1,0:T(8,128)(2,1)}), bf16[8,272,640]{2,1,0:T(8,128)(2,1)}, u32[]{:S(2)}, u32[]{:S(2)}) async-start(bf16[8,272,640]{2,1,0:T(8,128)(2,1)} %shard_map.138), calls=%async_computation.2 | async-start | bytes 5570560 | tf_op jit(solution)/shard_map/all_to_all | solution.py:407
  92.9 72.8 %all-gather.4.cloned.1.call-done = bf16[512,1536]{0,1:T(8,128)(2,1)} async-done(((bf16[512,192]{0,1:T(8,128)(2,1)}), bf16[512,1536]{0,1:T(8,128)(2,1)}) %all-gather.4.cloned.1.call-update) | async-done | bytes 1572880 | tf_op jit(solution)/shard_map/all_gather | solution.py:420
  168.6 49.0 %all-gather.8.cloned.1.call-done = bf16[768,1536]{0,1:T(8,128)(2,1)} async-done(((bf16[768,192]{0,1:T(8,128)(2,1)}), bf16[768,1536]{0,1:T(8,128)(2,1)}) %all-gather.8.cloned.1.call-update) | async-done | bytes 2359312 | tf_op jit(solution)/shard_map/all_gather | solution.py:420
  220.2 3.3 %slice_convert_fusion = f32[8,272,384]{2,1,0:T(8,128)} fusion(bf16[8,272,640]{2,1,0:T(8,128)(2,1)} %all-to-all-done.2), kind=kLoop, calls=%fused_computation.15 | loop fusion | flops 835584 | bytes 5013504 | tf_op jit(solution)/shard_map/convert_element_type | solution.py:432
  223.5 6.7 %reshape.101 = f32[8,272,2,192]{3,2,1,0:T(2,128)} reshape(f32[8,272,384]{2,1,0:T(8,128)} %slice_convert_fusion) | data formatting | bytes 6684672 | tf_op jit(solution)/shard_map/convert_element_type | solution.py:432
  230.2 6.9 %copy.18 = f32[2,272,8,192]{3,2,1,0:T(8,128)} copy(f32[2,272,8,192]{3,0,1,2:T(2,128)} %bitcast.43) | data formatting | bytes 6684672 | tf_op jit(solution)/shard_map/convert_element_type | solution.py:432
  237.1 5.3 %reshape.100 = f32[544,1536]{1,0:T(8,128)} reshape(f32[2,272,8,192]{3,2,1,0:T(8,128)} %copy.18) | data formatting | bytes 6684672 | tf_op jit(solution)/shard_map/convert_element_type | solution.py:432
  242.4 2.6 fusion.29
  245.0 2.6 fusion.43
  249.4 2.8 fusion.9
  252.2 4.9 %convolution_add_fusion = f32[544,3072]{1,0:T(8,128)S(1)} fusion(f32[544,3072]{1,0:T(8,128)S(1)} %fusion.9, bf16[768,3072]{1,0:T(8,128)(2,1)} %collective-permute-done.1, pred[]{:T(512)S(6)} %eq.95, bf16[544,1536]{1,0:T(8,128)(2,1)S(1)} %add_convert_fusion), kind=kOutput, calls=%fused_computation | convolution fusion | flops 2569003008 | bytes 19759104 | tf_op jit(solution)/shard_map/dot_general | solution.py:429
  257.1 2.1 fusion.5.gated_ref
  260.1 14.6 %shard_map.139 = bf16[512,1536]{1,0:T(8,128)(2,1)} custom-call(s32[8]{0:T(128)} %convert_element_type.36.uniform_ref, bf16[544,1536]{1,0:T(8,128)(2,1)} %fusion.5.gated_ref, s32[544,128]{1,0:T(8,128)} %broadcast_in_dim.113.segment_ref, f32[31,1536]{1,0:T(8,128)} %taps_ref.1, f32[1,1536]{1,0:T(1,128)} %broadcast_in_dim.114.scale_ref, ...), custom_call_target="tpu_custom_call" | custom-call | flops 48758784 | bytes 3145728 | tf_op jit(solution)/shard_map/pallas_call | solution.py:325
  274.7 3.7 %fusion.16 = f32[512,1536]{1,0:T(8,128)S(1)} fusion(bf16[768,1536]{0,1:T(8,128)(2,1)} %all-gather.8.cloned.1.call-done, pred[]{:T(512)S(6)} %eq.95, bf16[512,1536]{1,0:T(8,128)(2,1)} %shard_map.139), kind=kOutput, calls=%fused_computation.26 | convolution fusion | flops 1208352768 | bytes 7077889 | tf_op jit(solution)/shard_map/dot_general | solution.py:427
  278.4 4.3 %fusion.7 = bf16[512,1536]{1,0:T(8,128)(2,1)} fusion(f32[544,1536]{1,0:T(8,128)S(1)} %copy-done.3, pred[512]{0:T(512)(128)(4,1)S(1)} %slice_compare_fusion, f32[512,1536]{1,0:T(8,128)S(1)} %fusion.16, bf16[768,1536]{0,1:T(8,128)(2,1)} %collective-permute-done.2, pred[]{:T(512)S(6)} %eq.95, bf16[512,1536]{1,0:T(8,128)(2,1)S(1)} %copy-done.7), kind=kOutput, calls=%fused_computation.14 | convolution fusion | flops 1211498496 | bytes 11796993 | tf_op jit(solution)/shard_map/dot_general | solution.py:429
  (89 shorter events, 19.7 us)
Async XLA Ops:
  6.5 6.2 %copy-start.9 = (bf16[2048,2,128]{2,1,0:T(2,128)(2,1)S(1)}, bf16[2048,2,128]{2,1,0:T(2,128)(2,1)}, u32[]{:S(2)}) copy-start(bf16[2048,2,128]{2,1,0:T(2,128)(2,1)} %param.14) | copy-start | bytes 3145732
  6.5 7.3 %copy-start.10 = (bf16[2048,2,128]{2,1,0:T(2,128)(2,1)S(1)}, bf16[2048,2,128]{2,1,0:T(2,128)(2,1)}, u32[]{:S(2)}) copy-start(bf16[2048,2,128]{2,1,0:T(2,128)(2,1)} %param.16) | copy-start | bytes 3145732
  6.5 86.2 %all-gather.6.cloned.1.call-start = ((), (), s32[]{:S(2)}) async-start(), calls=%async_computation.4 | async-start | bytes 5308416 | tf_op jit(solution)/shard_map/all_gather | solution.py:420
  8.7 5.1 %copy-start.11 = (bf16[2048,2,128]{2,1,0:T(2,128)(2,1)S(1)}, bf16[2048,2,128]{2,1,0:T(2,128)(2,1)}, u32[]{:S(2)}) copy-start(bf16[2048,2,128]{2,1,0:T(2,128)(2,1)} %param.15) | copy-start | bytes 3145732
  8.8 157.0 %all-gather.4.cloned.1.call-start = ((), (), s32[]{:S(2)}) async-start(), calls=%async_computation.3 | async-start | bytes 1769472 | tf_op jit(solution)/shard_map/all_gather | solution.py:420
  12.8 2.8 copy-start.17
  16.3 23.6 %copy-start.8 = (bf16[1024,1,768]{2,0,1:T(8,128)(2,1)S(1)}, bf16[1024,1,768]{2,0,1:T(8,128)(2,1)}, u32[]{:S(2)}) copy-start(bf16[1024,1,768]{2,0,1:T(8,128)(2,1)} %param.17) | copy-start | bytes 4718596
  35.5 18.8 %all-to-all-start.1 = ((bf16[16,256,128]{2,1,0:T(8,128)(2,1)}), bf16[16,256,128]{2,1,0:T(8,128)(2,1)S(1)}, u32[]{:S(2)}, u32[]{:S(2)}) async-start(bf16[16,256,128]{2,1,0:T(8,128)(2,1)} %shard_map.137), calls=%async_computation.1 | async-start | bytes 2097152 | tf_op jit(solution)/shard_map/all_to_all | solution.py:407
  54.3 23.6 %copy-start.6 = (bf16[16,256,128]{2,1,0:T(8,128)(2,1)}, bf16[16,256,128]{2,1,0:T(8,128)(2,1)S(1)}, u32[]{:S(2)}) copy-start(bf16[16,256,128]{2,1,0:T(8,128)(2,1)S(1)} %all-to-all-done.1.context_ref) | copy-start | bytes 3145732
  54.3 23.6 %all-to-all-start = ((bf16[8,256,384]{2,1,0:T(8,128)(2,1)}), bf16[8,256,384]{2,1,0:T(8,128)(2,1)S(1)}, u32[]{:S(2)}, u32[]{:S(2)}) async-start(bf16[8,256,384]{2,1,0:T(8,128)(2,1)} %shard_map.136), calls=%async_computation | async-start | bytes 3145728 | tf_op jit(solution)/shard_map/all_to_all | solution.py:407
  84.4 6.7 %copy-start.12 = (bf16[1536,192]{0,1:T(8,128)(2,1)S(1)}, bf16[1536,192]{0,1:T(8,128)(2,1)}, u32[]{:S(2)}) copy-start(bf16[1536,192]{0,1:T(8,128)(2,1)} %param.27) | copy-start | bytes 1769476
  84.4 8.4 %copy-start.18 = (s32[17]{0:T(128)S(1)}, s32[17]{0:T(128)}, u32[]{:S(2)}) copy-start(s32[17]{0:T(128)} %select_reduce_fusion.1.after_ref) | copy-start | bytes 208
  84.4 83.0 %copy-start.15 = (f32[1536]{0:T(1024)S(1)}, f32[1536]{0:T(1024)}, u32[]{:S(2)}) copy-start(f32[1536]{0:T(1024)} %param.25) | copy-start | bytes 18436
  84.4 83.6 %copy-start.16 = (f32[1536]{0:T(1024)S(1)}, f32[1536]{0:T(1024)}, u32[]{:S(2)}) copy-start(f32[1536]{0:T(1024)} %param.26) | copy-start | bytes 18436
  84.4 133.3 %all-to-all-start.2 = ((bf16[8,272,640]{2,1,0:T(8,128)(2,1)}), bf16[8,272,640]{2,1,0:T(8,128)(2,1)}, u32[]{:S(2)}, u32[]{:S(2)}) async-start(bf16[8,272,640]{2,1,0:T(8,128)(2,1)} %shard_map.138), calls=%async_computation.2 | async-start | bytes 5570560 | tf_op jit(solution)/shard_map/all_to_all | solution.py:407
  91.0 126.6 %all-gather.8.cloned.1.call-start = ((), (), s32[]{:S(2)}) async-start(), calls=%async_computation.5 | async-start | bytes 2654208 | tf_op jit(solution)/shard_map/all_gather | solution.py:420
  92.7 159.4 %collective-permute-start.1 = (bf16[768,3072]{1,0:T(8,128)(2,1)}, bf16[768,3072]{1,0:T(8,128)(2,1)}, u32[]{:S(2)}, u32[]{:S(2)}) collective-permute-start(bf16[768,3072]{1,0:T(8,128)(2,1)} %all-gather.6.cloned.1.call-done), channel_id=1, source_target_pairs={{0,8},{8,0},{16,24},{24,16},{1,9},{9,1},{17,25},{25,17},{2,10},{10... | collective-permute-start | bytes 14155784 | tf_op jit(solution)/shard_map/ppermute | solution.py:421
  165.7 79.3 %collective-permute-start = (bf16[512,1536]{0,1:T(8,128)(2,1)}, bf16[512,1536]{0,1:T(8,128)(2,1)}, u32[]{:S(2)}, u32[]{:S(2)}) collective-permute-start(bf16[512,1536]{0,1:T(8,128)(2,1)} %all-gather.4.cloned.1.call-done), channel_id=1, source_target_pairs={{0,8},{8,0},{16,24},{24,16},{1,9},{9,1},{17,25},{25,17},{2,10},{10... | collective-permute-start | bytes 4718600 | tf_op jit(solution)/shard_map/ppermute | solution.py:421
  217.6 60.8 %collective-permute-start.2 = (bf16[768,1536]{0,1:T(8,128)(2,1)}, bf16[768,1536]{0,1:T(8,128)(2,1)}, u32[]{:S(2)}, u32[]{:S(2)}) collective-permute-start(bf16[768,1536]{0,1:T(8,128)(2,1)} %all-gather.8.cloned.1.call-done), channel_id=1, source_target_pairs={{0,8},{8,0},{16,24},{24,16},{1,9},{9,1},{17,25},{25,17},{2,10},{10... | collective-permute-start | bytes 7077896 | tf_op jit(solution)/shard_map/ppermute | solution.py:421
  242.4 7.0 %slice-start = ((s8[4718592]{0:T(1024)(128)(4,1)}), s8[4194304]{0:T(1024)(128)(4,1)S(1)}, s32[]{:S(2)}) async-start(s8[4718592]{0:T(1024)(128)(4,1)} %bitcast.51), calls=%async_computation.6 | async-start | bytes 8388608
  245.0 4.4 %slice-start.1 = ((s8[4718592]{0:T(1024)(128)(4,1)}), s8[524288]{0:T(1024)(128)(4,1)S(1)}, s32[]{:S(2)}) async-start(s8[4718592]{0:T(1024)(128)(4,1)} %bitcast.51), calls=%async_computation.7 | async-start | bytes 1048576
  274.7 3.7 %copy-start.3 = (f32[544,1536]{1,0:T(8,128)S(1)}, f32[544,1536]{1,0:T(8,128)}, u32[]{:S(2)}) copy-start(f32[544,1536]{1,0:T(8,128)} %copy-done.2) | copy-start | bytes 10027012
  274.7 3.8 %copy-start.7 = (bf16[512,1536]{1,0:T(8,128)(2,1)S(1)}, bf16[512,1536]{1,0:T(8,128)(2,1)}, u32[]{:S(2)}) copy-start(bf16[512,1536]{1,0:T(8,128)(2,1)} %shard_map.139) | copy-start | bytes 4718596
  274.7 8.1 %copy-start.1 = (bf16[1536,384]{1,0:T(8,128)(2,1)S(1)}, bf16[1536,384]{1,0:T(8,128)(2,1)}, u32[]{:S(2)}) copy-start(bf16[1536,384]{1,0:T(8,128)(2,1)} %param.23) | copy-start | bytes 3538948
  (6 other events, 8.3 us)
Sparse Core Ops, SparseCore 0:
  9.4 83.3 all-gather.5
  94.9 70.7 all-gather.3
  167.9 49.6 all-gather.7

commit v2 on v1

--- a/solution.py
+++ b/solution.py
@@ -261,21 +261,57 @@
     )(after, x_slots, context_slots)
 
 
+def unplace_kernel(moved_ref, x_ref, context_ref):
+    slabs, rows, _ = moved_ref.shape
+    step = 16
+    span = 3 * LANES
+
+    def chunk(index, carry):
+        at = pl.multiple_of(index * step, step)
+
+        def load(slab, tile):
+            cells = moved_ref[slab, pl.ds(at, step), tile * LANES : (tile + 1) * LANES]
+            return cells.astype(jnp.float32)
+
+        for pair in range(slabs // 2):
+            split = [
+                split_pair([load(2 * pair + member, tile) for tile in range(3)])
+                for member in range(2)
+            ]
+            for side in range(2):
+                to = pl.ds(pl.multiple_of(at + side * rows, step), step)
+                for tile, cells in enumerate(join_pair(split[0][side], split[1][side])):
+                    first = pair * span + tile * LANES
+                    x_ref[to, first : first + LANES] = cells.astype(jnp.bfloat16)
+        for slab in range(slabs):
+            for side in range(2):
+                to = pl.ds(pl.multiple_of(at + side * rows, step), step)
+                first = span + side * LANES
+                context_ref[to, slab * LANES : (slab + 1) * LANES] = moved_ref[
+                    slab, pl.ds(at, step), first : first + LANES
+                ]
+        return carry
+
+    lax.fori_loop(0, rows // step, chunk, 0)
+
+
 def unplace(moved, features, context_width):
     slabs, rows, _ = moved.shape
-    if not pairable(features):
+    if not (pairable(features) and context_width == LANES):
         first = len(lane_tiles(features)) * LANES
         x = moved[:, :, :features].transpose(1, 0, 2).reshape(rows, -1)
         context = moved[:, :, first : first + context_width]
         return x, context.transpose(1, 0, 2).reshape(rows, -1)
-
-    def sides(part, width):
-        return part.reshape(slabs, rows, 2, width).transpose(2, 1, 0, 3).reshape(2 * rows, -1)
-
-    return (
-        sides(moved[:, :, : 2 * features], features),
-        sides(moved[:, :, 2 * features :], context_width),
-    )
+    return pl.pallas_call(
+        unplace_kernel,
+        out_shape=(
+            jax.ShapeDtypeStruct((2 * rows, slabs * features), jnp.bfloat16),
+            jax.ShapeDtypeStruct((2 * rows, slabs * context_width), jnp.bfloat16),
+        ),
+        in_specs=[whole_spec()],
+        out_specs=(whole_spec(), whole_spec()),
+        compiler_params=params(),
+    )(moved)
 
 
 def conv_kernel(
@@ -406,7 +442,8 @@
     def swap(array, axis):
         return lax.all_to_all(array, axis, split_axis=0, concat_axis=0, tiled=True)
 
-    x_slots = swap(into_slots(start, residual_rows), "dp")
+    packed, start = lax.optimization_barrier((into_slots(start, residual_rows), start))
+    x_slots = swap(packed, "dp")
     context_slots = swap(attend(start, span, query_rows, key_rows, value_rows), "dp")
     moved = swap(place(after, x_slots, context_slots, slabs, slab_rows, features), "mp")
     carried_slab, context_slab = unplace(moved, features, query_rows.shape[1] * HD)
@@ -417,7 +454,9 @@
     def gather(weights):
         half = weights.shape[0] // 2
         own = lax.dynamic_slice_in_dim(weights, core * half, half, 0)
-        own = lax.all_gather(own, "mp", axis=1, tiled=True)
+        return lax.all_gather(own, "mp", axis=1, tiled=True)
+
+    def both(own):
         return own, lax.ppermute(own, "dp", partners)
 
     def project(rows, halves_of):
@@ -428,7 +467,8 @@
             jnp.where(core == 0, low, high), own, preferred_element_type=jnp.float32
         ) + jnp.dot(jnp.where(core == 0, high, low), other, preferred_element_type=jnp.float32)
 
-    out_halves, glu_halves, down_halves = gather(out_proj), gather(glu_proj), gather(down_proj)
+    out_halves, glu_halves = both(gather(out_proj)), both(gather(glu_proj))
+    down_own = gather(down_proj)
     carried = carried_slab.astype(jnp.float32) + project(context_slab, out_halves)
     average = jnp.mean(carried, axis=1, keepdims=True)
     centred = carried - average
@@ -439,6 +479,8 @@
     gated_rows = (halves[:, :feature_count] * jax.nn.sigmoid(halves[:, feature_count:])).astype(
         jnp.bfloat16
     )
+    down_own, gated_rows = lax.optimization_barrier((down_own, gated_rows))
+    down_halves = both(down_own)
     swished = convolve(gated_rows, segment, conv_taps, batch_scale, batch_shift)
     lowered = project(swished, down_halves)
     centre_segment = segment[HALO : HALO + slab_rows]

time: 291 us -> 257 us (0.88)
  waiting for transfers between devices: 150 us -> 118 us
  blocking collectives: 0 us -> 19.5 us
  local copies, waits for them, and re-layouts: 35.8 us -> 17.7 us
  Pallas kernels: 43.1 us -> 48.9 us
  other arithmetic: 11.7 us -> 7.02 us
  starting transfers between devices: 14.7 us -> 10.6 us
    all_gather x3, waiting for transfers between devices: 123 us -> 92.8 us  [gather(): return lax.all_gather(own, 'mp', axis=1, tiled=True)]
    all_to_all x0 -> x1, blocking collectives: none -> 19.5 us  [swap(): return lax.all_to_all(array, axis, split_axis=0, concat_axis=0, tiled=True)]
    convert_element_type x3 -> x0, local copies, waits for them, and re-layouts: 18.8 us -> none  [on_device(): carried_slab.astype(jnp.float32) + project(context_slab, out_halves)]
    pallas_call x0 -> x1, Pallas kernels: none -> 5.86 us  [unplace(): pl.pallas_call(unplace_kernel, out_shape=(jax.ShapeDtypeStruct((2 * rows,...]
    all_to_all x3 -> x2, starting transfers between devices: 14.6 us -> 10.3 us  [swap(): return lax.all_to_all(array, axis, split_axis=0, concat_axis=0, tiled=True)]
    convert_element_type x1 -> x0, other arithmetic: 3.34 us -> none  [on_device(): carried_slab.astype(jnp.float32) + project(context_slab, out_halves)]
    all_to_all x3 -> x2, waiting for transfers between devices: 26.7 us -> 25.6 us  [swap(): return lax.all_to_all(array, axis, split_axis=0, concat_axis=0, tiled=True)]
  transfers between devices with their start and end apart: 9 -> 8, of which waited for: 5 -> 4; matrix products, arithmetic and copies ran while one was open for 21% -> 14% of each run, Pallas kernels for 15% -> 19%
where the time goes in v2:
time: 257 us; the launch traced here: 255 us
  waiting for transfers between devices  118 us (46%)
  Pallas kernels  48.9 us (19%)
  matrix products  19.6 us (8%)
  blocking collectives  19.5 us (8%)
  local copies, waits for them, and re-layouts  17.7 us (7%)
  between operations  13.4 us (5%)
  starting transfers between devices  10.6 us (4%)
  other arithmetic  7.02 us (3%)
    all_gather x3, waiting for transfers between devices, gather(): return lax.all_gather(own, 'mp', axis=1, tiled=True)  92.8 us
    all_to_all x2, waiting for transfers between devices, swap(): return lax.all_to_all(array, axis, split_axis=0, concat_axis=0, tiled=True)  25.6 us
    all_to_all x1, blocking collectives, swap(): return lax.all_to_all(array, axis, split_axis=0, concat_axis=0, tiled=True)  19.5 us
    pallas_call x1, Pallas kernels, attend(): pl.pallas_call(functools.partial(attention_kernel, heads), out_shape=jax....  19.2 us
    pallas_call x1, Pallas kernels, convolve(): pl.pallas_call(conv_kernel, grid=(width // LANES,), out_shape=jax.ShapeDt...  14.6 us
    all_to_all x2, starting transfers between devices, swap(): return lax.all_to_all(array, axis, split_axis=0, concat_axis=0, tiled=True)  10.3 us
    dot_general x3, matrix products, project(): jnp.dot(jnp.where(core == 0, high, low), other, preferred_element_type=jn...  10.1 us
    dot_general x3, matrix products, project(): jnp.dot(jnp.where(core == 0, low, high), own, preferred_element_type=jnp....  9.46 us
  transfers between devices with their start and end apart: 8, of which 4 were waited for; matrix products, arithmetic and copies ran while one was open for 14% of the time, Pallas kernels for 19%

profile of v2, /device:TPU:0, one launch (start us, length us, event | category | flops | bytes accessed | tf_op | source)
XLA Modules:
  0.0 255.1 jit_solution(6087075123160505609)
XLA Ops:
  6.6 1.2 copy-done
  8.7 4.6 %reshape_reshape.3.rows_ref = bf16[4096,192]{1,0:T(8,128)(2,1)} reshape(bf16[1024,1,768]{2,0,1:T(8,128)(2,1)} %param.17) | data formatting | bytes 3145728 | tf_op jit(solution)/shard_map/reshape;reshape | solution.py:439
  14.9 4.0 %shard_map.136 = bf16[8,256,384]{2,1,0:T(8,128)(2,1)} custom-call(s32[16]{0:T(128)} %get-tuple-element.12.start_ref, bf16[4096,192]{1,0:T(8,128)(2,1)} %reshape_reshape.3.rows_ref), custom_call_target="tpu_custom_call" | custom-call | tf_op jit(solution)/shard_map/pallas_call | solution.py:177
  20.1 1.7 copy_bitcast_fusion
  21.8 19.2 %shard_map.137 = bf16[16,256,128]{2,1,0:T(8,128)(2,1)} custom-call(s32[16]{0:T(128)} %get-tuple-element.12.start_ref, s32[16]{0:T(128)} %get-tuple-element.17.span_ref, bf16[2048,256]{1,0:T(8,128)(2,1)} %bitcast.34, bf16[2048,256]{1,0:T(8,128)(2,1)} %get-tuple-element.35.k_ref, bf16[2048,256]{1,0:T(8,128)(2,1)} %get-tuple-element.34.v_ref), custom_call_target="tpu_custom_call" | custom-call | flops 1073741824 | bytes 4194304 | tf_op jit(solution)/shard_map/pallas_call | solution.py:98
  41.0 19.5 %all_to_all.15.context_ref = bf16[16,256,128]{2,1,0:T(8,128)(2,1)} all-to-all(bf16[16,256,128]{2,1,0:T(8,128)(2,1)} %shard_map.137), channel_id=1, replica_groups=mesh['dp'=4,'mp'=8] {'dp'}, dimensions={0} | all-to-all | bytes 2097152 | tf_op jit(solution)/shard_map/all_to_all | solution.py:443
  60.4 3.6 %all-to-all-start = ((bf16[8,256,384]{2,1,0:T(8,128)(2,1)}), bf16[8,256,384]{2,1,0:T(8,128)(2,1)S(1)}, u32[]{:S(2)}, u32[]{:S(2)}) async-start(bf16[8,256,384]{2,1,0:T(8,128)(2,1)} %shard_map.136), calls=%async_computation | async-start | bytes 3145728 | tf_op jit(solution)/shard_map/all_to_all | solution.py:443
  64.7 19.3 %all-to-all-done.x_ref = bf16[8,256,384]{2,1,0:T(8,128)(2,1)S(1)} async-done(((bf16[8,256,384]{2,1,0:T(8,128)(2,1)}), bf16[8,256,384]{2,1,0:T(8,128)(2,1)S(1)}, u32[]{:S(2)}, u32[]{:S(2)}) %all-to-all-start) | async-done | bytes 1572896 | tf_op jit(solution)/shard_map/all_to_all | solution.py:443
  85.2 5.3 %shard_map.138 = bf16[8,272,640]{2,1,0:T(8,128)(2,1)} custom-call(s32[17]{0:T(128)} %select_reduce_fusion.1.after_ref, bf16[8,256,384]{2,1,0:T(8,128)(2,1)} %copy-done.5, bf16[16,256,128]{2,1,0:T(8,128)(2,1)} %all_to_all.15.context_ref), custom_call_target="tpu_custom_call" | custom-call | tf_op jit(solution)/shard_map/pallas_call | solution.py:253
  90.4 6.7 %all-to-all-start.2 = ((bf16[8,272,640]{2,1,0:T(8,128)(2,1)}), bf16[8,272,640]{2,1,0:T(8,128)(2,1)S(1)}, u32[]{:S(2)}, u32[]{:S(2)}) async-start(bf16[8,272,640]{2,1,0:T(8,128)(2,1)} %shard_map.138), calls=%async_computation.2 | async-start | bytes 5570560 | tf_op jit(solution)/shard_map/all_to_all | solution.py:443
  97.2 1.6 constant_dynamic-slice_fusion
  99.2 72.9 %all-gather.4.cloned.1.call-done = bf16[512,1536]{0,1:T(8,128)(2,1)} async-done(((bf16[512,192]{0,1:T(8,128)(2,1)}), bf16[512,1536]{0,1:T(8,128)(2,1)}) %all-gather.4.cloned.1.call-update) | async-done | bytes 1572880 | tf_op jit(solution)/shard_map/all_gather | solution.py:457
  172.8 6.3 %all-to-all-done.2.moved_ref = bf16[8,272,640]{2,1,0:T(8,128)(2,1)S(1)} async-done(((bf16[8,272,640]{2,1,0:T(8,128)(2,1)}), bf16[8,272,640]{2,1,0:T(8,128)(2,1)S(1)}, u32[]{:S(2)}, u32[]{:S(2)}) %all-to-all-start.2) | async-done | bytes 2785312 | tf_op jit(solution)/shard_map/all_to_all | solution.py:443
  179.1 1.5 copy-done.4
  180.6 5.9 %shard_map.139 = (bf16[544,1536]{1,0:T(8,128)(2,1)}, bf16[544,1024]{1,0:T(8,128)(2,1)}) custom-call(bf16[8,272,640]{2,1,0:T(8,128)(2,1)} %copy-done.4), custom_call_target="tpu_custom_call" | custom-call | tf_op jit(solution)/shard_map/pallas_call | solution.py:305
  186.5 3.0 %fusion.29 = f32[544,1536]{1,0:T(8,128)S(1)} fusion(bf16[512,1536]{0,1:T(8,128)(2,1)} %all-gather.4.cloned.1.call-done, pred[]{:T(512)S(6)} %eq.95, bf16[544,1024]{1,0:T(8,128)(2,1)} %get-tuple-element.14), kind=kOutput, calls=%fused_computation.37 | convolution fusion | flops 855916544 | bytes 6029313 | tf_op jit(solution)/shard_map/dot_general | solution.py:466
  189.5 2.7 %fusion.43 = (f32[544]{0:T(1024)S(1)}, f32[544,1536]{1,0:T(8,128)S(1)}) fusion(f32[544,1536]{1,0:T(8,128)S(1)} %fusion.29, bf16[512,1536]{0,1:T(8,128)(2,1)} %collective-permute-done, pred[]{:T(512)S(6)} %eq.95, bf16[544,1024]{1,0:T(8,128)(2,1)S(1)} %copy-done.11, bf16[544,1536]{1,0:T(8,128)(2,1)S(1)} %copy-done.7), kind=kOutput, calls=%fused_computation.87 | convolution fusion | flops 859258368 | bytes 11044993 | tf_op jit(solution)/shard_map/dot_general | solution.py:468
  194.0 2.8 %fusion.9 = f32[544,3072]{1,0:T(8,128)S(1)} fusion(bf16[768,3072]{1,0:T(8,128)(2,1)S(1)} %bitcast.39, pred[]{:T(512)S(6)} %eq.95, bf16[544,1536]{1,0:T(8,128)(2,1)S(1)} %add_convert_fusion), kind=kOutput, calls=%fused_computation.19 | convolution fusion | flops 2567331840 | bytes 13074433 | tf_op jit(solution)/shard_map/dot_general | solution.py:466
  196.8 4.7 %convolution_add_fusion = f32[544,3072]{1,0:T(8,128)S(1)} fusion(f32[544,3072]{1,0:T(8,128)S(1)} %fusion.9, bf16[768,3072]{1,0:T(8,128)(2,1)} %collective-permute-done.1, pred[]{:T(512)S(6)} %eq.95, bf16[544,1536]{1,0:T(8,128)(2,1)S(1)} %add_convert_fusion), kind=kOutput, calls=%fused_computation | convolution fusion | flops 2569003008 | bytes 19759104 | tf_op jit(solution)/shard_map/dot_general | solution.py:468
  201.6 2.1 fusion.5.gated_ref
  203.7 19.9 %all-gather.6.cloned.1.call-done = bf16[768,1536]{0,1:T(8,128)(2,1)} async-done(((bf16[768,192]{0,1:T(8,128)(2,1)}), bf16[768,1536]{0,1:T(8,128)(2,1)}) %all-gather.6.cloned.1.call-update) | async-done | bytes 2359312 | tf_op jit(solution)/shard_map/all_gather | solution.py:457
  227.6 14.6 %shard_map.140 = bf16[512,1536]{1,0:T(8,128)(2,1)} custom-call(s32[8]{0:T(128)} %convert_element_type.24.uniform_ref, bf16[544,1536]{1,0:T(8,128)(2,1)} %fusion.5.gated_ref, s32[544,128]{1,0:T(8,128)} %broadcast_in_dim.113.segment_ref, f32[31,1536]{1,0:T(8,128)} %taps_ref.1, f32[1,1536]{1,0:T(1,128)} %broadcast_in_dim.114.scale_ref, ...), custom_call_target="tpu_custom_call" | custom-call | flops 48758784 | bytes 3145728 | tf_op jit(solution)/shard_map/pallas_call | solution.py:361
  242.2 3.7 %fusion.16 = f32[512,1536]{1,0:T(8,128)S(1)} fusion(bf16[768,1536]{0,1:T(8,128)(2,1)} %all-gather.6.cloned.1.call-done, pred[]{:T(512)S(6)} %eq.95, bf16[512,1536]{1,0:T(8,128)(2,1)} %shard_map.140), kind=kOutput, calls=%fused_computation.24 | convolution fusion | flops 1208352768 | bytes 7077889 | tf_op jit(solution)/shard_map/dot_general | solution.py:466
  245.9 2.7 %fusion.7 = bf16[512,1536]{1,0:T(8,128)(2,1)} fusion(f32[544,1536]{1,0:T(8,128)S(1)} %copy-done.3, pred[512]{0:T(512)(128)(4,1)S(1)} %slice_compare_fusion, f32[512,1536]{1,0:T(8,128)S(1)} %fusion.16, bf16[768,1536]{0,1:T(8,128)(2,1)S(1)} %collective-permute-done.2, pred[]{:T(512)S(6)} %eq.95, bf16[512,1536]{1,0:T(8,128)(2,1)S(1)} %copy-done.6), kind=kOutput, calls=%fused_computation.14 | convolution fusion | flops 1211498496 | bytes 11796993 | tf_op jit(solution)/shard_map/dot_general | solution.py:468
  (83 shorter events, 12.3 us)
Async XLA Ops:
  6.5 6.8 %copy-start.17 = (s32[64]{0:T(128)S(1)}, s32[64]{0:T(128)}, u32[]{:S(2)}) copy-start(s32[64]{0:T(128)} %param.18) | copy-start | bytes 772
  6.5 6.9 %copy-start.18 = (s32[64]{0:T(128)S(1)}, s32[64]{0:T(128)}, u32[]{:S(2)}) copy-start(s32[64]{0:T(128)} %param.19) | copy-start | bytes 772
  6.5 92.5 %all-gather.8.cloned.1.call-start = ((), (), s32[]{:S(2)}) async-start(), calls=%async_computation.5 | async-start | bytes 5308416 | tf_op jit(solution)/shard_map/all_gather | solution.py:457
  8.7 10.3 %copy-start.8 = (bf16[2048,2,128]{2,1,0:T(2,128)(2,1)S(1)}, bf16[2048,2,128]{2,1,0:T(2,128)(2,1)}, u32[]{:S(2)}) copy-start(bf16[2048,2,128]{2,1,0:T(2,128)(2,1)} %param.14) | copy-start | bytes 3145732
  13.4 6.7 %copy-start.9 = (bf16[2048,2,128]{2,1,0:T(2,128)(2,1)S(1)}, bf16[2048,2,128]{2,1,0:T(2,128)(2,1)}, u32[]{:S(2)}) copy-start(bf16[2048,2,128]{2,1,0:T(2,128)(2,1)} %param.16) | copy-start | bytes 3145732
  13.4 6.7 %copy-start.10 = (bf16[2048,2,128]{2,1,0:T(2,128)(2,1)S(1)}, bf16[2048,2,128]{2,1,0:T(2,128)(2,1)}, u32[]{:S(2)}) copy-start(bf16[2048,2,128]{2,1,0:T(2,128)(2,1)} %param.15) | copy-start | bytes 3145732
  60.4 23.6 %all-to-all-start = ((bf16[8,256,384]{2,1,0:T(8,128)(2,1)}), bf16[8,256,384]{2,1,0:T(8,128)(2,1)S(1)}, u32[]{:S(2)}, u32[]{:S(2)}) async-start(bf16[8,256,384]{2,1,0:T(8,128)(2,1)} %shard_map.136), calls=%async_computation | async-start | bytes 3145728 | tf_op jit(solution)/shard_map/all_to_all | solution.py:443
  90.4 81.6 %copy-start.12 = (bf16[1536,192]{0,1:T(8,128)(2,1)S(1)}, bf16[1536,192]{0,1:T(8,128)(2,1)}, u32[]{:S(2)}) copy-start(bf16[1536,192]{0,1:T(8,128)(2,1)} %param.27) | copy-start | bytes 1769476
  90.4 88.7 %all-to-all-start.2 = ((bf16[8,272,640]{2,1,0:T(8,128)(2,1)}), bf16[8,272,640]{2,1,0:T(8,128)(2,1)S(1)}, u32[]{:S(2)}, u32[]{:S(2)}) async-start(bf16[8,272,640]{2,1,0:T(8,128)(2,1)} %shard_map.138), calls=%async_computation.2 | async-start | bytes 5570560 | tf_op jit(solution)/shard_map/all_to_all | solution.py:443
  97.1 74.9 %all-gather.4.cloned.1.call-start = ((), (), s32[]{:S(2)}) async-start(), calls=%async_computation.3 | async-start | bytes 1769472 | tf_op jit(solution)/shard_map/all_gather | solution.py:457
  98.8 124.8 %all-gather.6.cloned.1.call-start = ((), (), s32[]{:S(2)}) async-start(), calls=%async_computation.4 | async-start | bytes 2654208 | tf_op jit(solution)/shard_map/all_gather | solution.py:457
  99.1 97.7 %collective-permute-start.1 = (bf16[768,3072]{1,0:T(8,128)(2,1)}, bf16[768,3072]{1,0:T(8,128)(2,1)}, u32[]{:S(2)}, u32[]{:S(2)}) collective-permute-start(bf16[768,3072]{1,0:T(8,128)(2,1)} %all-gather.8.cloned.1.call-done), channel_id=1, source_target_pairs={{0,8},{8,0},{16,24},{24,16},{1,9},{9,1},{17,25},{25,17},{2,10},{10... | collective-permute-start | bytes 14155784 | tf_op jit(solution)/shard_map/ppermute | solution.py:460
  172.0 17.5 %collective-permute-start = (bf16[512,1536]{0,1:T(8,128)(2,1)}, bf16[512,1536]{0,1:T(8,128)(2,1)}, u32[]{:S(2)}, u32[]{:S(2)}) collective-permute-start(bf16[512,1536]{0,1:T(8,128)(2,1)} %all-gather.4.cloned.1.call-done), channel_id=1, source_target_pairs={{0,8},{8,0},{16,24},{24,16},{1,9},{9,1},{17,25},{25,17},{2,10},{10... | collective-permute-start | bytes 4718600 | tf_op jit(solution)/shard_map/ppermute | solution.py:460
  186.5 3.0 %copy-start.7 = (bf16[544,1536]{1,0:T(8,128)(2,1)S(1)}, bf16[544,1536]{1,0:T(8,128)(2,1)}, u32[]{:S(2)}) copy-start(bf16[544,1536]{1,0:T(8,128)(2,1)} %get-tuple-element.13) | copy-start | bytes 5013508
  186.5 3.0 %copy-start.11 = (bf16[544,1024]{1,0:T(8,128)(2,1)S(1)}, bf16[544,1024]{1,0:T(8,128)(2,1)}, u32[]{:S(2)}) copy-start(bf16[544,1024]{1,0:T(8,128)(2,1)} %get-tuple-element.14) | copy-start | bytes 3342340
  186.5 7.5 %slice-start = ((s8[4718592]{0:T(1024)(128)(4,1)}), s8[4194304]{0:T(1024)(128)(4,1)S(1)}, s32[]{:S(2)}) async-start(s8[4718592]{0:T(1024)(128)(4,1)} %bitcast.38), calls=%async_computation.6 | async-start | bytes 8388608
  189.5 4.5 %slice-start.1 = ((s8[4718592]{0:T(1024)(128)(4,1)}), s8[524288]{0:T(1024)(128)(4,1)S(1)}, s32[]{:S(2)}) async-start(s8[4718592]{0:T(1024)(128)(4,1)} %bitcast.38), calls=%async_computation.7 | async-start | bytes 1048576
  201.6 22.1 %copy-start.19 = (s32[17]{0:T(128)S(1)}, s32[17]{0:T(128)}, u32[]{:S(2)}) copy-start(s32[17]{0:T(128)} %select_reduce_fusion.1.after_ref) | copy-start | bytes 208
  201.6 23.9 %copy-start.15 = (f32[1536]{0:T(1024)S(1)}, f32[1536]{0:T(1024)}, u32[]{:S(2)}) copy-start(f32[1536]{0:T(1024)} %param.25) | copy-start | bytes 18436
  201.6 24.5 %copy-start.16 = (f32[1536]{0:T(1024)S(1)}, f32[1536]{0:T(1024)}, u32[]{:S(2)}) copy-start(f32[1536]{0:T(1024)} %param.26) | copy-start | bytes 18436
  223.7 22.2 %collective-permute-start.2 = (bf16[768,1536]{0,1:T(8,128)(2,1)}, bf16[768,1536]{0,1:T(8,128)(2,1)S(1)}, u32[]{:S(2)}, u32[]{:S(2)}) collective-permute-start(bf16[768,1536]{0,1:T(8,128)(2,1)} %all-gather.6.cloned.1.call-done), channel_id=1, source_target_pairs={{0,8},{8,0},{16,24},{24,16},{1,9},{9,1},{17,25},{25,17},{2,10},{10... | collective-permute-start | bytes 7077896 | tf_op jit(solution)/shard_map/ppermute | solution.py:460
  242.2 3.7 %copy-start.3 = (f32[544,1536]{1,0:T(8,128)S(1)}, f32[544,1536]{1,0:T(8,128)}, u32[]{:S(2)}) copy-start(f32[544,1536]{1,0:T(8,128)} %copy-done.2) | copy-start | bytes 10027012
  242.2 3.8 %copy-start.6 = (bf16[512,1536]{1,0:T(8,128)(2,1)S(1)}, bf16[512,1536]{1,0:T(8,128)(2,1)}, u32[]{:S(2)}) copy-start(bf16[512,1536]{1,0:T(8,128)(2,1)} %shard_map.140) | copy-start | bytes 4718596
  242.2 6.4 %copy-start.1 = (bf16[1536,384]{1,0:T(8,128)(2,1)S(1)}, bf16[1536,384]{1,0:T(8,128)(2,1)}, u32[]{:S(2)}) copy-start(bf16[1536,384]{1,0:T(8,128)(2,1)} %param.23) | copy-start | bytes 3538948
  (6 other events, 7.2 us)
Sparse Core Ops, SparseCore 0:
  9.4 83.3 all-gather.7
  100.1 71.8 all-gather.3
  174.2 49.3 all-gather.5
